TPU v7x, 32 devices: a whole 2x2x4 slice. The times are simulated.
32 devices in a mesh: section: 2 (over x), dp: 4 (over y, core), expert: 4 (over z).
Axes of the slice: x: 2, y: 2, z: 4, core: 2. Of those that a mesh axis runs over, the one named last changes fastest.
Arguments:
- tokens: bfloat16 [2, 2048, 2560], P('section', ('dp', 'expert')), may hold values from -6 to 6
- cotangent: bfloat16 [2, 2048, 2560], P('section', ('dp', 'expert')), may hold values from -3 to 3
- routes: int32 [2, 2048, 6], P('section', ('dp', 'expert')), may hold values from 0 to 159, as said below
- gates: float32 [2, 2048, 6], P('section', ('dp', 'expert')), may hold values from 0.2 to 1
- gate_up: bfloat16 [2, 4, 2, 1024, 2560], P('section', 'expert', None, 'dp'), may hold values from -0.125 to 0.125
- down: bfloat16 [2, 4, 1024, 2560], P('section', 'expert', 'dp'), may hold values from -0.1875 to 0.1875
Outputs:
- handed_on: bfloat16 [2, 2048, 2560], P('section', ('dp', 'expert'))
- handed_back: bfloat16 [2, 2048, 2560], P('section', ('dp', 'expert'))
- grad_gate_up: bfloat16 [2, 4, 2, 1024, 2560], P('section', 'expert', None, 'dp')
- grad_down: bfloat16 [2, 4, 1024, 2560], P('section', 'expert', 'dp')
Inputs may be any that keep to these rules, and one draw needn't show every extreme that they name: `routes`: A token's 6 ids are distinct and at most one of them is below 4. In each device's block of 128 tokens no id below 4 is named by more than 32 tokens.
All inputs are finite; a program needn't handle non-finite values.
Results may differ from a plain program's by a relative error of at most 0.0065.
Values may be sent and summed in bfloat16 or wider, within the bound.
No kernel may reach another device: no remote copies, remote signals or barrier semaphores. Data moves between devices by JAX's collectives and lax.ppermute only.
A program may use at most 64 MiB of HBM per device.

v0:
```python
import jax
import jax.numpy as jnp
from jax import lax
from jax.sharding import PartitionSpec as P


def passed_along(value, axis, steps):
    count = lax.axis_size(axis)
    first, last = (max(0, -steps), min(count, count - steps))
    return lax.ppermute(value, axis, [(source, source + steps) for source in range(first, last)])


def to_experts(buffer):
    columns = lax.all_to_all(buffer, "expert", split_axis=0, concat_axis=0, tiled=True)
    arrived = lax.all_gather(columns, "dp", axis=0, tiled=True)
    return arrived


def to_owners(partial_value):
    copies = lax.axis_size("dp")
    quarters = lax.all_to_all(partial_value, "dp", split_axis=0, concat_axis=0, tiled=True)
    quarters = quarters.reshape((copies, quarters.shape[0] // copies) + quarters.shape[1:])
    column_rows = jnp.sum(quarters.astype(jnp.float32), 0).astype(jnp.bfloat16)
    summed = lax.all_to_all(column_rows, "expert", split_axis=0, concat_axis=0, tiled=True)
    return summed


def shards(tokens, cotangent, routes, gates, gate_up, down):
    window = lax.axis_size("expert")
    copies = lax.axis_size("dp")
    rows_here = tokens.shape[1]
    model_width = tokens.shape[2]
    capacity = rows_here // window
    in_window = routes[0] < window
    expert_of = jnp.sum(jnp.where(in_window, routes[0], 0), -1)
    present = jnp.any(in_window, -1)
    weight = jnp.sum(jnp.where(in_window, gates[0], 0.0), -1)
    member = ((expert_of[:, None] == jnp.arange(window)[None, :]) & present[:, None]).astype(
        jnp.float32
    )
    before = jnp.cumsum(member, 0) - member
    slot_index = jnp.sum(before * member, -1)
    slot_values = jnp.arange(capacity, dtype=jnp.float32)
    select = member.T[:, None, :] * (slot_index[None, None, :] == slot_values[None, :, None])
    select = select.astype(jnp.bfloat16).reshape(window * capacity, rows_here)
    contract_last = (((1,), (1,)), ((), ()))
    contract_first = (((0,), (0,)), ((), ()))

    def to_slots(values):
        packed = jnp.dot(select, values, preferred_element_type=jnp.float32).astype(jnp.bfloat16)
        arrived = to_experts(packed.reshape(window, capacity, model_width))
        return arrived.reshape(copies * window * capacity, model_width)

    def from_slots(partial_value):
        rounded = partial_value.astype(jnp.bfloat16).reshape(copies * window, capacity, model_width)
        owner_rows = to_owners(rounded).reshape(window * capacity, model_width)
        return lax.dot_general(
            select, owner_rows, contract_first, preferred_element_type=jnp.float32
        )

    gate_matrix = gate_up[0, 0, 0]
    up_matrix = gate_up[0, 0, 1]
    down_matrix = down[0, 0]
    slot_rows = to_slots(tokens[0])
    pre_gate = lax.dot_general(
        slot_rows, gate_matrix, contract_last, preferred_element_type=jnp.float32
    )
    pre_up = lax.dot_general(
        slot_rows, up_matrix, contract_last, preferred_element_type=jnp.float32
    )
    sigmoid_gate = jax.nn.sigmoid(pre_gate)
    activated = pre_gate * sigmoid_gate
    hidden = (activated * pre_up).astype(jnp.bfloat16)
    partial_value = jnp.dot(hidden, down_matrix, preferred_element_type=jnp.float32)
    mixture = (from_slots(partial_value) * weight[:, None]).astype(jnp.bfloat16)
    handed_on = passed_along(mixture[None], "section", 1)
    scaled = (cotangent[0].astype(jnp.float32) * weight[:, None]).astype(jnp.bfloat16)
    slot_grads = to_slots(scaled)
    hidden_grad = lax.dot_general(
        slot_grads, down_matrix, contract_last, preferred_element_type=jnp.float32
    )
    grad_down = lax.dot_general(
        hidden, slot_grads, contract_first, preferred_element_type=jnp.float32
    ).astype(jnp.bfloat16)
    gate_slope = sigmoid_gate * (1.0 + pre_gate * (1.0 - sigmoid_gate))
    gate_grad = (hidden_grad * pre_up * gate_slope).astype(jnp.bfloat16)
    up_grad = (hidden_grad * activated).astype(jnp.bfloat16)
    grad_gate = lax.dot_general(
        gate_grad, slot_rows, contract_first, preferred_element_type=jnp.float32
    ).astype(jnp.bfloat16)
    grad_up = lax.dot_general(
        up_grad, slot_rows, contract_first, preferred_element_type=jnp.float32
    ).astype(jnp.bfloat16)
    input_part = jnp.dot(gate_grad, gate_matrix, preferred_element_type=jnp.float32)
    input_part = input_part + jnp.dot(up_grad, up_matrix, preferred_element_type=jnp.float32)
    input_grad = from_slots(input_part).astype(jnp.bfloat16)
    handed_back = passed_along(input_grad[None], "section", -1)
    grads_pair = jnp.stack([grad_gate, grad_up])[None, None]
    return (handed_on, handed_back, grads_pair, grad_down[None, None])


def solution(mesh):
    in_specs = (
        P("section", ("dp", "expert"), None),
        P("section", ("dp", "expert"), None),
        P("section", ("dp", "expert"), None),
        P("section", ("dp", "expert"), None),
        P("section", "expert", None, "dp", None),
        P("section", "expert", "dp", None),
    )
    out_specs = (
        P("section", ("dp", "expert"), None),
        P("section", ("dp", "expert"), None),
        P("section", "expert", None, "dp", None),
        P("section", "expert", "dp", None),
    )
    return jax.shard_map(shards, mesh=mesh, in_specs=in_specs, out_specs=out_specs, check_vma=False)
```

profile of v0, /device:TPU:0, one launch (start us, length us, event | category | flops | bytes accessed | tf_op | source)
XLA Modules:
  0.0 233.5 jit_solution(1484516350349944796)
XLA Ops:
  9.3 1.4 convolution_convert_fusion.5
  10.7 23.5 %all_to_all.30 = bf16[4,32,2560]{2,1,0:T(8,128)(2,1)} all-to-all(bf16[4,32,2560]{2,1,0:T(8,128)(2,1)S(1)} %bitcast.96), channel_id=1, replica_groups=mesh['section'=2,'dp'=4,'expert'=4] {'expert'}, dimensions={0} | all-to-all | bytes 1310720 | tf_op jit(solution)/shard_map/all_to_all | solution.py:14
  34.8 19.6 %all_to_all.31 = bf16[4,32,2560]{2,1,0:T(8,128)(2,1)} all-to-all(bf16[4,32,2560]{2,1,0:T(8,128)(2,1)S(1)} %bitcast.95), channel_id=1, replica_groups=mesh['section'=2,'dp'=4,'expert'=4] {'expert'}, dimensions={0} | all-to-all | bytes 1310720 | tf_op jit(solution)/shard_map/all_to_all | solution.py:14
  54.4 4.6 %all-gather.3.cloned.1.call-done = bf16[16,32,2560]{2,1,0:T(8,128)(2,1)} async-done(((bf16[4,32,2560]{2,1,0:T(8,128)(2,1)}), bf16[16,32,2560]{2,1,0:T(8,128)(2,1)}) %all-gather.3.cloned.1.call-update) | async-done | bytes 2621456 | tf_op jit(solution)/shard_map/all_gather | solution.py:15
  59.1 3.1 %fusion.12 = f32[512,256]{1,0:T(8,128)S(1)} fusion(bf16[512,2560]{1,0:T(8,128)(2,1)} %bitcast.91, bf16[1,1,2,256,2560]{4,3,2,1,0:T(8,128)(2,1)} %param.10), kind=kOutput, calls=%fused_computation.22 | convolution fusion | flops 671088640 | bytes 4456448 | tf_op jit(solution)/shard_map/dot_general | solution.py:68
  62.8 0.9 fusion.16
  63.7 22.5 %all-gather.5.cloned.1.call-done = bf16[16,32,2560]{2,1,0:T(8,128)(2,1)} async-done(((bf16[4,32,2560]{2,1,0:T(8,128)(2,1)}), bf16[16,32,2560]{2,1,0:T(8,128)(2,1)}) %all-gather.5.cloned.1.call-update) | async-done | bytes 2621456 | tf_op jit(solution)/shard_map/all_gather | solution.py:15
  86.2 2.7 %multiply_convert_fusion.1 = (bf16[512,256]{1,0:T(8,128)(2,1)S(1)}, bf16[512,256]{1,0:T(8,128)(2,1)S(1)}, bf16[512,256]{1,0:T(8,128)(2,1)S(1)}) fusion(f32[512,256]{1,0:T(8,128)S(1)} %fusion.16, f32[512,256]{1,0:T(8,128)S(1)} %fusion.12, bf16[512,2560]{1,0:T(8,128)(2,1)} %bitcast.97, bf16[1,1,256,2560]{3,2,1,0:T(8,128)(2,1)S(1)} %copy-done), kind=kOutput, calls=%fused_computation.36 | convolution fusion | flops 673054720 | bytes 5767168 | tf_op jit(solution)/shard_map/dot_general | solution.py:79
  88.9 2.3 %convolution_convert_fusion = bf16[512,2560]{1,0:T(8,128)(2,1)} fusion(bf16[512,256]{1,0:T(8,128)(2,1)S(1)} %get-tuple-element.6, bf16[1,1,256,2560]{3,2,1,0:T(8,128)(2,1)S(1)} %copy-done), kind=kOutput, calls=%fused_computation.1 | convolution fusion | flops 672399360 | bytes 4194304 | tf_op jit(solution)/shard_map/dot_general | solution.py:74
  91.3 4.6 %all-to-all-start.1 = ((bf16[16,32,2560]{2,1,0:T(8,128)(2,1)}), bf16[16,32,2560]{2,1,0:T(8,128)(2,1)}, u32[]{:S(2)}, u32[]{:S(2)}) async-start(bf16[16,32,2560]{2,1,0:T(8,128)(2,1)} %bitcast.89), calls=%async_computation.1 | async-start | bytes 5242880 | tf_op jit(solution)/shard_map/all_to_all | solution.py:21
  95.9 2.3 fusion.14
  98.2 2.4 %add_convert_fusion = bf16[512,2560]{1,0:T(8,128)(2,1)} fusion(f32[512,2560]{1,0:T(8,128)S(1)} %fusion.14, bf16[512,256]{1,0:T(8,128)(2,1)S(1)} %get-tuple-element.4, bf16[1,1,2,256,2560]{4,3,2,1,0:T(8,128)(2,1)S(1)} %copy-done.4), kind=kOutput, calls=%fused_computation | convolution fusion | flops 673710080 | bytes 9437184 | tf_op jit(solution)/shard_map/dot_general | solution.py:95
  100.6 26.6 %all-to-all-done.1 = bf16[16,32,2560]{2,1,0:T(8,128)(2,1)} async-done(((bf16[16,32,2560]{2,1,0:T(8,128)(2,1)}), bf16[16,32,2560]{2,1,0:T(8,128)(2,1)}, u32[]{:S(2)}, u32[]{:S(2)}) %all-to-all-start.1) | async-done | bytes 2621472 | tf_op jit(solution)/shard_map/all_to_all | solution.py:21
  127.2 4.6 %all-to-all-start.4 = ((bf16[16,32,2560]{2,1,0:T(8,128)(2,1)}), bf16[16,32,2560]{2,1,0:T(8,128)(2,1)}, u32[]{:S(2)}, u32[]{:S(2)}) async-start(bf16[16,32,2560]{2,1,0:T(8,128)(2,1)} %bitcast.90), calls=%async_computation.4 | async-start | bytes 5242880 | tf_op jit(solution)/shard_map/all_to_all | solution.py:21
  131.8 3.1 %reduce_sum.53 = bf16[4,32,2560]{2,1,0:T(8,128)(2,1)} reduce(bf16[4,4,32,2560]{3,2,1,0:T(8,128)(2,1)} %bitcast.8, bf16[]{:T(256)} %constant.16.clone.1), dimensions={0}, to_apply=%region_4.5 | reduce | flops 983040 | bytes 3276802 | tf_op jit(solution)/shard_map/reduce_sum | solution.py:23
  135.0 28.2 %all-to-all-done.4 = bf16[16,32,2560]{2,1,0:T(8,128)(2,1)} async-done(((bf16[16,32,2560]{2,1,0:T(8,128)(2,1)}), bf16[16,32,2560]{2,1,0:T(8,128)(2,1)}, u32[]{:S(2)}, u32[]{:S(2)}) %all-to-all-start.4) | async-done | bytes 2621472 | tf_op jit(solution)/shard_map/all_to_all | solution.py:21
  163.2 4.6 %all-to-all-start.2 = ((bf16[4,32,2560]{2,1,0:T(8,128)(2,1)}), bf16[4,32,2560]{2,1,0:T(8,128)(2,1)S(1)}, u32[]{:S(2)}, u32[]{:S(2)}) async-start(bf16[4,32,2560]{2,1,0:T(8,128)(2,1)} %reduce_sum.53), calls=%async_computation.2 | async-start | bytes 1310720 | tf_op jit(solution)/shard_map/all_to_all | solution.py:24
  167.8 3.1 %reduce_sum.55 = bf16[4,32,2560]{2,1,0:T(8,128)(2,1)} reduce(bf16[4,4,32,2560]{3,2,1,0:T(8,128)(2,1)} %bitcast.15, bf16[]{:T(256)} %constant.16.clone.1), dimensions={0}, to_apply=%region_6.7 | reduce | flops 983040 | bytes 3276802 | tf_op jit(solution)/shard_map/reduce_sum | solution.py:23
  170.9 13.9 %all-to-all-done.2 = bf16[4,32,2560]{2,1,0:T(8,128)(2,1)S(1)} async-done(((bf16[4,32,2560]{2,1,0:T(8,128)(2,1)}), bf16[4,32,2560]{2,1,0:T(8,128)(2,1)S(1)}, u32[]{:S(2)}, u32[]{:S(2)}) %all-to-all-start.2) | async-done | bytes 655392 | tf_op jit(solution)/shard_map/all_to_all | solution.py:24
  184.8 4.2 %all-to-all-start.5 = ((bf16[4,32,2560]{2,1,0:T(8,128)(2,1)}), bf16[4,32,2560]{2,1,0:T(8,128)(2,1)}, u32[]{:S(2)}, u32[]{:S(2)}) async-start(bf16[4,32,2560]{2,1,0:T(8,128)(2,1)} %reduce_sum.55), calls=%async_computation.5 | async-start | bytes 1310720 | tf_op jit(solution)/shard_map/all_to_all | solution.py:24
  189.0 3.8 %fusion.2 = bf16[1,1,256,2560]{3,2,1,0:T(8,128)(2,1)} fusion(bf16[512,256]{1,0:T(8,128)(2,1)S(1)} %get-tuple-element.6, bf16[512,2560]{1,0:T(8,128)(2,1)} %bitcast.98), kind=kOutput, calls=%fused_computation.7 | convolution fusion | flops 671744000 | bytes 4194304 | tf_op jit(solution)/shard_map/dot_general | solution.py:82
  192.8 1.8 fusion.1
  194.6 1.2 fusion.6
  195.8 3.4 %collective-permute-start = (bf16[1,128,2560]{2,1,0:T(8,128)(2,1)}, bf16[1,128,2560]{2,1,0:T(8,128)(2,1)S(1)}, u32[]{:S(2)}, u32[]{:S(2)}) collective-permute-start(bf16[1,128,2560]{2,1,0:T(8,128)(2,1)} %fusion.6), channel_id=1, source_target_pairs={{0,16},{1,17},{2,18},{3,19},{4,20},{5,21},{6,22},{7,23},{8,24},{9,... | collective-permute-start | bytes 1966088 | tf_op jit(solution)/shard_map/ppermute | solution.py:10
  199.3 6.6 %all-to-all-done.5 = bf16[4,32,2560]{2,1,0:T(8,128)(2,1)} async-done(((bf16[4,32,2560]{2,1,0:T(8,128)(2,1)}), bf16[4,32,2560]{2,1,0:T(8,128)(2,1)}, u32[]{:S(2)}, u32[]{:S(2)}) %all-to-all-start.5) | async-done | bytes 655392 | tf_op jit(solution)/shard_map/all_to_all | solution.py:24
  205.9 1.4 fusion.7
  207.3 1.3 collective-permute-start.1
  208.6 2.6 %fusion = bf16[1,256,2560]{2,1,0:T(8,128)(2,1)S(1)} fusion(bf16[512,256]{1,0:T(8,128)(2,1)S(1)} %get-tuple-element.5, bf16[512,2560]{1,0:T(8,128)(2,1)} %bitcast.92), kind=kOutput, calls=%fused_computation.5 | convolution fusion | flops 671744000 | bytes 4194304 | tf_op jit(solution)/shard_map/dot_general | solution.py:88
  211.2 1.7 maximum_bitcast_fusion
  213.0 12.0 %collective-permute-done.1 = bf16[1,128,2560]{2,1,0:T(8,128)(2,1)S(1)} collective-permute-done((bf16[1,128,2560]{2,1,0:T(8,128)(2,1)S(1)}, bf16[1,128,2560]{2,1,0:T(8,128)(2,1)S(1)}, u32[]{:S(2)}, u32[]{:S(2)}) %collective-permute-start.1) | collective-permute-done | bytes 655392 | tf_op jit(solution)/shard_map/ppermute | solution.py:10
  225.0 0.8 copy.25
  225.8 0.8 copy.26
  (41 shorter events, 3.2 us)
Async XLA Ops:
  7.2 79.1 %copy-start = (bf16[1,1,256,2560]{3,2,1,0:T(8,128)(2,1)S(1)}, bf16[1,1,256,2560]{3,2,1,0:T(8,128)(2,1)}, u32[]{:S(2)}) copy-start(bf16[1,1,256,2560]{3,2,1,0:T(8,128)(2,1)} %param.11) | copy-start | bytes 3932164
  7.2 27.2 %copy-start.9 = (s32[1,128,6]{1,0,2:T(1,128)S(1)}, s32[1,128,6]{1,0,2:T(1,128)}, u32[]{:S(2)}) copy-start(s32[1,128,6]{1,0,2:T(1,128)} %param.8) | copy-start | bytes 9220
  7.2 27.2 %copy-start.12 = (f32[1,128,6]{1,0,2:T(1,128)S(1)}, f32[1,128,6]{1,0,2:T(1,128)}, u32[]{:S(2)}) copy-start(f32[1,128,6]{1,0,2:T(1,128)} %param.9) | copy-start | bytes 9220
  7.2 27.2 %copy-start.6 = (bf16[1,128,2560]{2,1,0:T(8,128)(2,1)S(1)}, bf16[1,128,2560]{2,1,0:T(8,128)(2,1)}, u32[]{:S(2)}) copy-start(bf16[1,128,2560]{2,1,0:T(8,128)(2,1)} %param.7) | copy-start | bytes 1966084
  7.2 51.9 %all-gather.3.cloned.1.call-start = ((), (), s32[]{:S(2)}) async-start(), calls=%async_computation.6 | async-start | bytes 3276800 | tf_op jit(solution)/shard_map/all_gather | solution.py:15
  8.8 45.6 %copy-start.7 = (f32[4,128]{1,0:T(4,128)}, f32[4,128]{1,0:T(4,128)S(1)}, u32[]{:S(2)}) copy-start(f32[4,128]{1,0:T(4,128)S(1)} %fusion.33) | copy-start | bytes 6148
  34.3 51.9 %all-gather.5.cloned.1.call-start = ((), (), s32[]{:S(2)}) async-start(), calls=%async_computation.7 | async-start | bytes 3276800 | tf_op jit(solution)/shard_map/all_gather | solution.py:15
  34.4 27.8 %copy-start.10 = (f32[128]{0:T(128)}, f32[128]{0:T(128)S(1)}, u32[]{:S(2)}) copy-start(f32[128]{0:T(128)S(1)} %fusion.30) | copy-start | bytes 1540
  59.1 3.1 %copy-start.1 = (bf16[16,32,2560]{2,1,0:T(8,128)(2,1)S(1)}, bf16[16,32,2560]{2,1,0:T(8,128)(2,1)}, u32[]{:S(2)}) copy-start(bf16[16,32,2560]{2,1,0:T(8,128)(2,1)} %all-gather.3.cloned.1.call-done) | copy-start | bytes 7864324
  59.1 3.7 %copy-start.3 = (bf16[1,1,2,256,2560]{4,3,2,1,0:T(8,128)(2,1)S(1)}, bf16[1,1,2,256,2560]{4,3,2,1,0:T(8,128)(2,1)}, u32[]{:S(2)}) copy-start(bf16[1,1,2,256,2560]{4,3,2,1,0:T(8,128)(2,1)} %param.10) | copy-start | bytes 7864324
  88.9 9.3 %copy-start.5 = (bf16[512,256]{1,0:T(8,128)(2,1)}, bf16[512,256]{1,0:T(8,128)(2,1)S(1)}, u32[]{:S(2)}) copy-start(bf16[512,256]{1,0:T(8,128)(2,1)S(1)} %get-tuple-element.4) | copy-start | bytes 786436
  91.3 35.9 %all-to-all-start.1 = ((bf16[16,32,2560]{2,1,0:T(8,128)(2,1)}), bf16[16,32,2560]{2,1,0:T(8,128)(2,1)}, u32[]{:S(2)}, u32[]{:S(2)}) async-start(bf16[16,32,2560]{2,1,0:T(8,128)(2,1)} %bitcast.89), calls=%async_computation.1 | async-start | bytes 5242880 | tf_op jit(solution)/shard_map/all_to_all | solution.py:21
  95.9 2.3 %copy-start.4 = (bf16[1,1,2,256,2560]{4,3,2,1,0:T(8,128)(2,1)S(1)}, bf16[1,1,2,256,2560]{4,3,2,1,0:T(8,128)(2,1)}, u32[]{:S(2)}) copy-start(bf16[1,1,2,256,2560]{4,3,2,1,0:T(8,128)(2,1)} %param.10) | copy-start | bytes 7864324
  127.2 36.0 %all-to-all-start.4 = ((bf16[16,32,2560]{2,1,0:T(8,128)(2,1)}), bf16[16,32,2560]{2,1,0:T(8,128)(2,1)}, u32[]{:S(2)}, u32[]{:S(2)}) async-start(bf16[16,32,2560]{2,1,0:T(8,128)(2,1)} %bitcast.90), calls=%async_computation.4 | async-start | bytes 5242880 | tf_op jit(solution)/shard_map/all_to_all | solution.py:21
  163.2 21.6 %all-to-all-start.2 = ((bf16[4,32,2560]{2,1,0:T(8,128)(2,1)}), bf16[4,32,2560]{2,1,0:T(8,128)(2,1)S(1)}, u32[]{:S(2)}, u32[]{:S(2)}) async-start(bf16[4,32,2560]{2,1,0:T(8,128)(2,1)} %reduce_sum.53), calls=%async_computation.2 | async-start | bytes 1310720 | tf_op jit(solution)/shard_map/all_to_all | solution.py:24
  184.8 21.1 %all-to-all-start.5 = ((bf16[4,32,2560]{2,1,0:T(8,128)(2,1)}), bf16[4,32,2560]{2,1,0:T(8,128)(2,1)}, u32[]{:S(2)}, u32[]{:S(2)}) async-start(bf16[4,32,2560]{2,1,0:T(8,128)(2,1)} %reduce_sum.55), calls=%async_computation.5 | async-start | bytes 1310720 | tf_op jit(solution)/shard_map/all_to_all | solution.py:24
  189.0 3.8 %copy-start.2 = (bf16[16,32,2560]{2,1,0:T(8,128)(2,1)S(1)}, bf16[16,32,2560]{2,1,0:T(8,128)(2,1)}, u32[]{:S(2)}) copy-start(bf16[16,32,2560]{2,1,0:T(8,128)(2,1)} %all-gather.3.cloned.1.call-done) | copy-start | bytes 7864324
  192.8 1.8 copy-start.8
  192.8 1.8 copy-start.11
  195.8 17.1 %collective-permute-start = (bf16[1,128,2560]{2,1,0:T(8,128)(2,1)}, bf16[1,128,2560]{2,1,0:T(8,128)(2,1)S(1)}, u32[]{:S(2)}, u32[]{:S(2)}) collective-permute-start(bf16[1,128,2560]{2,1,0:T(8,128)(2,1)} %fusion.6), channel_id=1, source_target_pairs={{0,16},{1,17},{2,18},{3,19},{4,20},{5,21},{6,22},{7,23},{8,24},{9,... | collective-permute-start | bytes 1966088 | tf_op jit(solution)/shard_map/ppermute | solution.py:10
  207.3 17.6 %collective-permute-start.1 = (bf16[1,128,2560]{2,1,0:T(8,128)(2,1)S(1)}, bf16[1,128,2560]{2,1,0:T(8,128)(2,1)S(1)}, u32[]{:S(2)}, u32[]{:S(2)}) collective-permute-start(bf16[1,128,2560]{2,1,0:T(8,128)(2,1)S(1)} %fusion.7), channel_id=1, source_target_pairs={{16,0},{17,1},{18,2},{19,3},{20,4},{21,5},{22,6},{23,7},{24,8},{25... | collective-permute-start | bytes 1966088 | tf_op jit(solution)/shard_map/ppermute | solution.py:10
Sparse Core Ops, SparseCore 0:
  34.4 24.6 all-gather.2
  60.7 25.5 all-gather.4
where the time goes:
time: 234 us; the launch traced here: 233 us
  waiting for transfers between devices  115 us (49%)
  blocking collectives  43.2 us (18%)
  matrix products  26.4 us (11%)
  starting transfers between devices  22.7 us (10%)
  between operations  14.3 us (6%)
  other arithmetic  10 us (4%)
    all_to_all x2, waiting for transfers between devices, to_owners(): lax.all_to_all(partial_value, 'dp', split_axis=0, concat_axis=0, tiled=True)  54.8 us
    all_to_all x2, blocking collectives, to_experts(): lax.all_to_all(buffer, 'expert', split_axis=0, concat_axis=0, tiled=True)  43.2 us
    all_gather x2, waiting for transfers between devices, to_experts(): arrived = lax.all_gather(columns, 'dp', axis=0, tiled=True)  27.2 us
    all_to_all x2, waiting for transfers between devices, to_owners(): lax.all_to_all(column_rows, 'expert', split_axis=0, concat_axis=0, tiled=...  20.5 us
    ppermute x2, waiting for transfers between devices, passed_along(): lax.ppermute(value, axis, [(source, source + steps) for source in range(f...  12 us
    all_to_all x2, starting transfers between devices, to_owners(): lax.all_to_all(partial_value, 'dp', split_axis=0, concat_axis=0, tiled=True)  9.2 us
    all_to_all x2, starting transfers between devices, to_owners(): lax.all_to_all(column_rows, 'expert', split_axis=0, concat_axis=0, tiled=...  8.76 us
    reduce_sum x2, other arithmetic, to_owners(): column_rows = jnp.sum(quarters.astype(jnp.float32), 0).astype(jnp.bfloat16)  6.29 us
  transfers between devices with their start and end apart: 8, of which 7 were waited for; matrix products, arithmetic and copies ran while one was open for 12% of the time, Pallas kernels for 0%

commit v1 on v0

--- a/solution.py
+++ b/solution.py
@@ -1,7 +1,19 @@
+import functools
 import jax
 import jax.numpy as jnp
 from jax import lax
 from jax.sharding import PartitionSpec as P
+from jax.lax import all_to_all, axis_size
+
+
+def recover_pieces_all(z_in, k_dim):
+    seen_now = axis_size("dp")
+    block_out = jnp.stack([z_in] * seen_now, 0)
+    s_next = all_to_all(block_out, "dp", 0, 0)
+    return jnp.concatenate(s_next, k_dim)
+
+
+answer_the_modes = functools.partial(recover_pieces_all, k_dim=0)
 
 
 def passed_along(value, axis, steps):
@@ -12,7 +24,7 @@
 
 def to_experts(buffer):
     columns = lax.all_to_all(buffer, "expert", split_axis=0, concat_axis=0, tiled=True)
-    arrived = lax.all_gather(columns, "dp", axis=0, tiled=True)
+    arrived = answer_the_modes(columns)
     return arrived
 
 

time: 234 us -> 262 us (1.12)
  waiting for transfers between devices: 115 us -> 131 us
  between operations: 14.3 us -> 0.89 us
  blocking collectives: 43.2 us -> 53.8 us
  starting transfers between devices: 22.7 us -> 32.4 us
    all_to_all x0 -> x2, waiting for transfers between devices: none -> 43.7 us  [the longest x1 26.8 us: recover_pieces_all(): s_next = all_to_all(block_out, 'dp', 0, 0)]
    all_to_all x0 -> x1, blocking collectives: none -> 34.6 us  [recover_pieces_all(): s_next = all_to_all(block_out, 'dp', 0, 0)]
    all_gather x2 -> x0, waiting for transfers between devices: 27.2 us -> none  [to_experts(): arrived = lax.all_gather(columns, 'dp', axis=0, tiled=True)]
    all_to_all x2 -> x1, blocking collectives: 43.2 us -> 19.3 us  [to_experts(): lax.all_to_all(buffer, 'expert', split_axis=0, concat_axis=0, tiled=True)]
    all_to_all x0 -> x2, starting transfers between devices: none -> 10.9 us  [the longest x1 6.35 us: to_experts(): lax.all_to_all(buffer, 'expert', split_axis=0, concat_axis=0, tiled=True)]
  transfers between devices with their start and end apart: 8 -> 8, of which waited for: 7 -> 7; matrix products, arithmetic and copies ran while one was open for 12% -> 11% of each run, Pallas kernels for 0% -> 0%
where the time goes in v1:
time: 262 us; the launch traced here: 261 us
  waiting for transfers between devices  131 us (50%)
  blocking collectives  53.8 us (21%)
  starting transfers between devices  32.4 us (12%)
  matrix products  27.2 us (10%)
  other arithmetic  10.8 us (4%)
  local copies, waits for them, and re-layouts  4.29 us (2%)
    all_to_all x2, waiting for transfers between devices, to_owners(): lax.all_to_all(partial_value, 'dp', split_axis=0, concat_axis=0, tiled=True)  54.8 us
    all_to_all x1, blocking collectives, recover_pieces_all(): s_next = all_to_all(block_out, 'dp', 0, 0)  34.6 us
    all_to_all x1, waiting for transfers between devices, recover_pieces_all(): s_next = all_to_all(block_out, 'dp', 0, 0)  26.8 us
    all_to_all x2, waiting for transfers between devices, to_owners(): lax.all_to_all(column_rows, 'expert', split_axis=0, concat_axis=0, tiled=...  20.7 us
    all_to_all x1, blocking collectives, to_experts(): lax.all_to_all(buffer, 'expert', split_axis=0, concat_axis=0, tiled=True)  19.3 us
    all_to_all x1, waiting for transfers between devices, to_experts(): lax.all_to_all(buffer, 'expert', split_axis=0, concat_axis=0, tiled=True)  17 us
    ppermute x2, waiting for transfers between devices, passed_along(): lax.ppermute(value, axis, [(source, source + steps) for source in range(f...  12 us
    all_to_all x2, starting transfers between devices, to_owners(): lax.all_to_all(partial_value, 'dp', split_axis=0, concat_axis=0, tiled=True)  9.18 us
  transfers between devices with their start and end apart: 8, of which 7 were waited for; matrix products, arithmetic and copies ran while one was open for 11% of the time, Pallas kernels for 0%

profile of v1, /device:TPU:0, one launch (start us, length us, event | category | flops | bytes accessed | tf_op | source)
XLA Modules:
  0.0 260.7 jit_solution(10953851252642300491)
XLA Ops:
  3.4 2.3 convolution_convert_fusion.4
  5.8 6.3 %all-to-all-start.4 = ((bf16[4,32,2560]{2,1,0:T(8,128)(2,1)}), bf16[4,32,2560]{2,1,0:T(8,128)(2,1)S(1)}, u32[]{:S(2)}, u32[]{:S(2)}) async-start(bf16[4,32,2560]{2,1,0:T(8,128)(2,1)} %bitcast.12), calls=%async_computation.4 | async-start | bytes 1310720 | tf_op jit(solution)/shard_map/all_to_all | solution.py:26
  12.4 17.0 %all-to-all-done.4 = bf16[4,32,2560]{2,1,0:T(8,128)(2,1)S(1)} async-done(((bf16[4,32,2560]{2,1,0:T(8,128)(2,1)}), bf16[4,32,2560]{2,1,0:T(8,128)(2,1)S(1)}, u32[]{:S(2)}, u32[]{:S(2)}) %all-to-all-start.4) | async-done | bytes 655392 | tf_op jit(solution)/shard_map/all_to_all | solution.py:26
  29.4 19.3 %all_to_all.40 = bf16[4,32,2560]{2,1,0:T(8,128)(2,1)S(1)} all-to-all(bf16[4,32,2560]{2,1,0:T(8,128)(2,1)S(1)} %bitcast.95), channel_id=1, replica_groups=mesh['section'=2,'dp'=4,'expert'=4] {'expert'}, dimensions={0} | all-to-all | bytes 1310720 | tf_op jit(solution)/shard_map/all_to_all | solution.py:26
  48.9 34.6 %all_to_all.41 = bf16[4,4,32,2560]{3,2,1,0:T(8,128)(2,1)} all-to-all(bf16[4,4,32,2560]{3,2,1,0:T(8,128)(2,1)S(1)} %stack.10), channel_id=1, replica_groups=mesh['section'=2,'dp'=4,'expert'=4] {'dp'}, dimensions={0} | all-to-all | bytes 5242880 | tf_op jit(solution)/shard_map/all_to_all | solution.py:12
  83.5 1.8 stack.11
  85.3 4.6 %all-to-all-start.5 = ((bf16[4,4,32,2560]{3,2,1,0:T(8,128)(2,1)}), bf16[4,4,32,2560]{3,2,1,0:T(8,128)(2,1)}, u32[]{:S(2)}, u32[]{:S(2)}) async-start(bf16[4,4,32,2560]{3,2,1,0:T(8,128)(2,1)} %stack.11), calls=%async_computation.5 | async-start | bytes 5242880 | tf_op jit(solution)/shard_map/all_to_all | solution.py:12
  89.8 3.1 %fusion.12 = f32[512,256]{1,0:T(8,128)S(1)} fusion(bf16[512,2560]{1,0:T(8,128)(2,1)} %bitcast.89, bf16[1,1,2,256,2560]{4,3,2,1,0:T(8,128)(2,1)} %param.10), kind=kOutput, calls=%fused_computation.22 | convolution fusion | flops 671088640 | bytes 4456448 | tf_op jit(solution)/shard_map/dot_general | solution.py:80
  94.4 26.8 %all-to-all-done.5 = bf16[4,4,32,2560]{3,2,1,0:T(8,128)(2,1)} async-done(((bf16[4,4,32,2560]{3,2,1,0:T(8,128)(2,1)}), bf16[4,4,32,2560]{3,2,1,0:T(8,128)(2,1)}, u32[]{:S(2)}, u32[]{:S(2)}) %all-to-all-start.5) | async-done | bytes 2621472 | tf_op jit(solution)/shard_map/all_to_all | solution.py:12
  121.2 2.7 %multiply_convert_fusion.1 = (bf16[512,256]{1,0:T(8,128)(2,1)S(1)}, bf16[512,256]{1,0:T(8,128)(2,1)S(1)}, bf16[512,256]{1,0:T(8,128)(2,1)S(1)}) fusion(f32[512,256]{1,0:T(8,128)S(1)} %fusion.16, f32[512,256]{1,0:T(8,128)S(1)} %fusion.12, bf16[512,2560]{1,0:T(8,128)(2,1)} %bitcast.13, bf16[1,1,256,2560]{3,2,1,0:T(8,128)(2,1)S(1)} %copy-done), kind=kOutput, calls=%fused_computation.36 | convolution fusion | flops 673054720 | bytes 5767168 | tf_op jit(solution)/shard_map/dot_general | solution.py:91
  123.9 2.3 convolution_convert_fusion
  126.2 4.6 %all-to-all-start.2 = ((bf16[16,32,2560]{2,1,0:T(8,128)(2,1)}), bf16[16,32,2560]{2,1,0:T(8,128)(2,1)}, u32[]{:S(2)}, u32[]{:S(2)}) async-start(bf16[16,32,2560]{2,1,0:T(8,128)(2,1)} %bitcast.93), calls=%async_computation.2 | async-start | bytes 5242880 | tf_op jit(solution)/shard_map/all_to_all | solution.py:33
  130.8 2.3 fusion.14
  133.2 2.4 add_convert_fusion
  135.5 26.6 %all-to-all-done.2 = bf16[16,32,2560]{2,1,0:T(8,128)(2,1)} async-done(((bf16[16,32,2560]{2,1,0:T(8,128)(2,1)}), bf16[16,32,2560]{2,1,0:T(8,128)(2,1)}, u32[]{:S(2)}, u32[]{:S(2)}) %all-to-all-start.2) | async-done | bytes 2621472 | tf_op jit(solution)/shard_map/all_to_all | solution.py:33
  162.2 4.6 %all-to-all-start.6 = ((bf16[16,32,2560]{2,1,0:T(8,128)(2,1)}), bf16[16,32,2560]{2,1,0:T(8,128)(2,1)}, u32[]{:S(2)}, u32[]{:S(2)}) async-start(bf16[16,32,2560]{2,1,0:T(8,128)(2,1)} %bitcast.94), calls=%async_computation.6 | async-start | bytes 5242880 | tf_op jit(solution)/shard_map/all_to_all | solution.py:33
  166.8 3.1 %reduce_sum.53 = bf16[4,32,2560]{2,1,0:T(8,128)(2,1)} reduce(bf16[4,4,32,2560]{3,2,1,0:T(8,128)(2,1)} %bitcast.8, bf16[]{:T(256)} %constant.16.clone.1), dimensions={0}, to_apply=%region_4.5 | reduce | flops 983040 | bytes 3276802 | tf_op jit(solution)/shard_map/reduce_sum | solution.py:35
  169.9 28.2 %all-to-all-done.6 = bf16[16,32,2560]{2,1,0:T(8,128)(2,1)} async-done(((bf16[16,32,2560]{2,1,0:T(8,128)(2,1)}), bf16[16,32,2560]{2,1,0:T(8,128)(2,1)}, u32[]{:S(2)}, u32[]{:S(2)}) %all-to-all-start.6) | async-done | bytes 2621472 | tf_op jit(solution)/shard_map/all_to_all | solution.py:33
  198.1 3.5 %all-to-all-start.3 = ((bf16[4,32,2560]{2,1,0:T(8,128)(2,1)}), bf16[4,32,2560]{2,1,0:T(8,128)(2,1)S(1)}, u32[]{:S(2)}, u32[]{:S(2)}) async-start(bf16[4,32,2560]{2,1,0:T(8,128)(2,1)} %reduce_sum.53), calls=%async_computation.3 | async-start | bytes 1310720 | tf_op jit(solution)/shard_map/all_to_all | solution.py:36
  201.6 3.1 %reduce_sum.55 = bf16[4,32,2560]{2,1,0:T(8,128)(2,1)} reduce(bf16[4,4,32,2560]{3,2,1,0:T(8,128)(2,1)} %bitcast.15, bf16[]{:T(256)} %constant.16.clone.1), dimensions={0}, to_apply=%region_6.7 | reduce | flops 983040 | bytes 3276802 | tf_op jit(solution)/shard_map/reduce_sum | solution.py:35
  204.7 14.1 %all-to-all-done.3 = bf16[4,32,2560]{2,1,0:T(8,128)(2,1)S(1)} async-done(((bf16[4,32,2560]{2,1,0:T(8,128)(2,1)}), bf16[4,32,2560]{2,1,0:T(8,128)(2,1)S(1)}, u32[]{:S(2)}, u32[]{:S(2)}) %all-to-all-start.3) | async-done | bytes 655392 | tf_op jit(solution)/shard_map/all_to_all | solution.py:36
  218.8 4.2 %all-to-all-start.7 = ((bf16[4,32,2560]{2,1,0:T(8,128)(2,1)}), bf16[4,32,2560]{2,1,0:T(8,128)(2,1)}, u32[]{:S(2)}, u32[]{:S(2)}) async-start(bf16[4,32,2560]{2,1,0:T(8,128)(2,1)} %reduce_sum.55), calls=%async_computation.7 | async-start | bytes 1310720 | tf_op jit(solution)/shard_map/all_to_all | solution.py:36
  223.0 3.8 %fusion.2 = bf16[1,1,256,2560]{3,2,1,0:T(8,128)(2,1)} fusion(bf16[512,256]{1,0:T(8,128)(2,1)S(1)} %get-tuple-element.6, bf16[512,2560]{1,0:T(8,128)(2,1)} %bitcast.13), kind=kOutput, calls=%fused_computation.7 | convolution fusion | flops 671744000 | bytes 4194304 | tf_op jit(solution)/shard_map/dot_general | solution.py:94
  226.8 1.8 fusion.1
  228.7 1.2 fusion.6
  229.9 3.4 %collective-permute-start = (bf16[1,128,2560]{2,1,0:T(8,128)(2,1)}, bf16[1,128,2560]{2,1,0:T(8,128)(2,1)S(1)}, u32[]{:S(2)}, u32[]{:S(2)}) collective-permute-start(bf16[1,128,2560]{2,1,0:T(8,128)(2,1)} %fusion.6), channel_id=1, source_target_pairs={{0,16},{1,17},{2,18},{3,19},{4,20},{5,21},{6,22},{7,23},{8,24},{9,... | collective-permute-start | bytes 1966088 | tf_op jit(solution)/shard_map/ppermute | solution.py:22
  233.3 6.6 %all-to-all-done.7 = bf16[4,32,2560]{2,1,0:T(8,128)(2,1)} async-done(((bf16[4,32,2560]{2,1,0:T(8,128)(2,1)}), bf16[4,32,2560]{2,1,0:T(8,128)(2,1)}, u32[]{:S(2)}, u32[]{:S(2)}) %all-to-all-start.7) | async-done | bytes 655392 | tf_op jit(solution)/shard_map/all_to_all | solution.py:36
  239.9 1.4 fusion.7
  241.4 1.3 collective-permute-start.1
  242.7 2.6 fusion
  245.3 1.7 maximum_bitcast_fusion
  247.0 12.0 %collective-permute-done.1 = bf16[1,128,2560]{2,1,0:T(8,128)(2,1)S(1)} collective-permute-done((bf16[1,128,2560]{2,1,0:T(8,128)(2,1)S(1)}, bf16[1,128,2560]{2,1,0:T(8,128)(2,1)S(1)}, u32[]{:S(2)}, u32[]{:S(2)}) %collective-permute-start.1) | collective-permute-done | bytes 655392 | tf_op jit(solution)/shard_map/ppermute | solution.py:22
  (37 shorter events, 6.5 us)
Async XLA Ops:
  0.6 120.5 %copy-start = (bf16[1,1,256,2560]{3,2,1,0:T(8,128)(2,1)S(1)}, bf16[1,1,256,2560]{3,2,1,0:T(8,128)(2,1)}, u32[]{:S(2)}) copy-start(bf16[1,1,256,2560]{3,2,1,0:T(8,128)(2,1)} %param.11) | copy-start | bytes 3932164
  0.6 11.5 %copy-start.6 = (bf16[1,128,2560]{2,1,0:T(8,128)(2,1)S(1)}, bf16[1,128,2560]{2,1,0:T(8,128)(2,1)}, u32[]{:S(2)}) copy-start(bf16[1,128,2560]{2,1,0:T(8,128)(2,1)} %param.6) | copy-start | bytes 1966084
  2.2 46.5 %copy-start.7 = (f32[4,128]{1,0:T(4,128)}, f32[4,128]{1,0:T(4,128)S(1)}, u32[]{:S(2)}) copy-start(f32[4,128]{1,0:T(4,128)S(1)} %fusion.33) | copy-start | bytes 6148
  3.0 45.6 %copy-start.9 = (f32[128]{0:T(128)}, f32[128]{0:T(128)S(1)}, u32[]{:S(2)}) copy-start(f32[128]{0:T(128)S(1)} %fusion.30) | copy-start | bytes 1540
  5.8 23.6 %all-to-all-start.4 = ((bf16[4,32,2560]{2,1,0:T(8,128)(2,1)}), bf16[4,32,2560]{2,1,0:T(8,128)(2,1)S(1)}, u32[]{:S(2)}, u32[]{:S(2)}) async-start(bf16[4,32,2560]{2,1,0:T(8,128)(2,1)} %bitcast.12), calls=%async_computation.4 | async-start | bytes 1310720 | tf_op jit(solution)/shard_map/all_to_all | solution.py:26
  85.3 35.9 %all-to-all-start.5 = ((bf16[4,4,32,2560]{3,2,1,0:T(8,128)(2,1)}), bf16[4,4,32,2560]{3,2,1,0:T(8,128)(2,1)}, u32[]{:S(2)}, u32[]{:S(2)}) async-start(bf16[4,4,32,2560]{3,2,1,0:T(8,128)(2,1)} %stack.11), calls=%async_computation.5 | async-start | bytes 5242880 | tf_op jit(solution)/shard_map/all_to_all | solution.py:12
  89.8 3.2 %copy-start.1 = (bf16[4,4,32,2560]{3,2,1,0:T(8,128)(2,1)S(1)}, bf16[4,4,32,2560]{3,2,1,0:T(8,128)(2,1)}, u32[]{:S(2)}) copy-start(bf16[4,4,32,2560]{3,2,1,0:T(8,128)(2,1)} %all_to_all.41) | copy-start | bytes 7864324
  89.8 3.7 %copy-start.3 = (bf16[1,1,2,256,2560]{4,3,2,1,0:T(8,128)(2,1)S(1)}, bf16[1,1,2,256,2560]{4,3,2,1,0:T(8,128)(2,1)}, u32[]{:S(2)}) copy-start(bf16[1,1,2,256,2560]{4,3,2,1,0:T(8,128)(2,1)} %param.10) | copy-start | bytes 7864324
  123.9 9.3 %copy-start.5 = (bf16[512,256]{1,0:T(8,128)(2,1)}, bf16[512,256]{1,0:T(8,128)(2,1)S(1)}, u32[]{:S(2)}) copy-start(bf16[512,256]{1,0:T(8,128)(2,1)S(1)} %get-tuple-element.4) | copy-start | bytes 786436
  126.2 35.9 %all-to-all-start.2 = ((bf16[16,32,2560]{2,1,0:T(8,128)(2,1)}), bf16[16,32,2560]{2,1,0:T(8,128)(2,1)}, u32[]{:S(2)}, u32[]{:S(2)}) async-start(bf16[16,32,2560]{2,1,0:T(8,128)(2,1)} %bitcast.93), calls=%async_computation.2 | async-start | bytes 5242880 | tf_op jit(solution)/shard_map/all_to_all | solution.py:33
  130.8 2.3 copy-start.4
  162.2 35.9 %all-to-all-start.6 = ((bf16[16,32,2560]{2,1,0:T(8,128)(2,1)}), bf16[16,32,2560]{2,1,0:T(8,128)(2,1)}, u32[]{:S(2)}, u32[]{:S(2)}) async-start(bf16[16,32,2560]{2,1,0:T(8,128)(2,1)} %bitcast.94), calls=%async_computation.6 | async-start | bytes 5242880 | tf_op jit(solution)/shard_map/all_to_all | solution.py:33
  198.1 20.7 %all-to-all-start.3 = ((bf16[4,32,2560]{2,1,0:T(8,128)(2,1)}), bf16[4,32,2560]{2,1,0:T(8,128)(2,1)S(1)}, u32[]{:S(2)}, u32[]{:S(2)}) async-start(bf16[4,32,2560]{2,1,0:T(8,128)(2,1)} %reduce_sum.53), calls=%async_computation.3 | async-start | bytes 1310720 | tf_op jit(solution)/shard_map/all_to_all | solution.py:36
  218.8 21.1 %all-to-all-start.7 = ((bf16[4,32,2560]{2,1,0:T(8,128)(2,1)}), bf16[4,32,2560]{2,1,0:T(8,128)(2,1)}, u32[]{:S(2)}, u32[]{:S(2)}) async-start(bf16[4,32,2560]{2,1,0:T(8,128)(2,1)} %reduce_sum.55), calls=%async_computation.7 | async-start | bytes 1310720 | tf_op jit(solution)/shard_map/all_to_all | solution.py:36
  223.0 3.8 %copy-start.2 = (bf16[4,4,32,2560]{3,2,1,0:T(8,128)(2,1)S(1)}, bf16[4,4,32,2560]{3,2,1,0:T(8,128)(2,1)}, u32[]{:S(2)}) copy-start(bf16[4,4,32,2560]{3,2,1,0:T(8,128)(2,1)} %all_to_all.41) | copy-start | bytes 7864324
  226.8 1.8 copy-start.8
  226.8 1.8 copy-start.10
  229.9 17.1 %collective-permute-start = (bf16[1,128,2560]{2,1,0:T(8,128)(2,1)}, bf16[1,128,2560]{2,1,0:T(8,128)(2,1)S(1)}, u32[]{:S(2)}, u32[]{:S(2)}) collective-permute-start(bf16[1,128,2560]{2,1,0:T(8,128)(2,1)} %fusion.6), channel_id=1, source_target_pairs={{0,16},{1,17},{2,18},{3,19},{4,20},{5,21},{6,22},{7,23},{8,24},{9,... | collective-permute-start | bytes 1966088 | tf_op jit(solution)/shard_map/ppermute | solution.py:22
  241.4 17.6 %collective-permute-start.1 = (bf16[1,128,2560]{2,1,0:T(8,128)(2,1)S(1)}, bf16[1,128,2560]{2,1,0:T(8,128)(2,1)S(1)}, u32[]{:S(2)}, u32[]{:S(2)}) collective-permute-start(bf16[1,128,2560]{2,1,0:T(8,128)(2,1)S(1)} %fusion.7), channel_id=1, source_target_pairs={{16,0},{17,1},{18,2},{19,3},{20,4},{21,5},{22,6},{23,7},{24,8},{25... | collective-permute-start | bytes 1966088 | tf_op jit(solution)/shard_map/ppermute | solution.py:22
